TPU v7x, 256 devices: a whole 4x4x8 slice. The times are simulated.
256 devices in a mesh: cable: 32 (over y_lo, z, core), grid: 8 (over x, y_hi).
Axes of the slice: x: 4, y: 4 (y_hi: 2, y_lo: 2; y = y_hi * 2 + y_lo), z: 8, core: 2. Of those that a mesh axis runs over, the one named last changes fastest.
Arguments:
- green: bfloat16 [2, 8192, 16384], P(None, 'cable', 'grid'), may hold values from -6 to 6
- source_weight: float32 [16384], P('grid'), may hold values from 0.25 to 4
- observed: float32 [2, 2, 8192, 256], P(None, None, 'cable'), may hold values from -6 to 6
- amp_weight: float32 [2, 8192, 256], P(None, 'cable'), may hold values from 0.25 to 2
- pair_used: int32 [32, 2], P('cable'), may hold values 0 or 1
Outputs:
- adjoint: float32 [2, 8192, 16384], P(None, 'cable', 'grid')
- kernel: float32 [16384], P('grid')
All inputs are finite; a program needn't handle non-finite values. No bound on the sum of `pair_used` on one device may be relied on, other than what follows from the above.
Results may differ from a plain program's by a relative error of at most 0.0037.
Values may be sent and summed in bfloat16 or wider, within the bound.
No kernel may reach another device: no remote copies, remote signals or barrier semaphores. Data moves between devices by JAX's collectives and lax.ppermute only.
A program may use at most 64 MiB of HBM per device.

v0:
```python
import math
import jax
import jax.numpy as jnp
from jax import lax
from jax.sharding import PartitionSpec as P


def shifted(block, axis, distance):
    devices = range(lax.axis_size(axis))
    route = [((i - distance) % len(devices), i) for i in devices]
    return lax.ppermute(block, axis, route)


def build_block(pair_resid):
    resid_real = pair_resid[0]
    resid_imag = pair_resid[1]
    upper_half = jnp.concatenate([resid_real, resid_imag], axis=1)
    lower_half = jnp.concatenate([-resid_imag, resid_real], axis=1)
    return jnp.concatenate([upper_half, lower_half], axis=0)


def residuals(corr, observed_rows, weight_rows, pair_used):
    mask_values = pair_used[0].astype(jnp.float32)
    scaled = mask_values[:, None, None, None] * weight_rows[:, None, :, :] * (corr - observed_rows)
    return scaled.astype(jnp.bfloat16)


def shards(green, source_weight, observed, amp_weight, pair_used):
    row_count = green.shape[1]
    col_count = green.shape[2]
    block_count = lax.axis_size("cable")
    grid_count = lax.axis_size("grid")
    inv_norm = 1.0 / math.sqrt(col_count * grid_count)
    kernel_scale = inv_norm / (2.0 * math.sqrt(2.0 * block_count))
    own_block = green.reshape(2 * row_count, col_count)
    near_blocks = []
    for offset in range(2):
        near_blocks.append(shifted(own_block, "cable", offset + 1))
    weighted = (own_block.astype(jnp.float32) * source_weight[None, :]).astype(jnp.bfloat16)
    partial_list = []
    for offset in range(2):
        products = lax.dot_general(
            weighted,
            near_blocks[offset],
            (((1,), (1,)), ((), ())),
            preferred_element_type=jnp.float32,
        )
        corr_real = products[:row_count, :row_count] + products[row_count:, row_count:]
        corr_imag = products[:row_count, row_count:] - products[row_count:, :row_count]
        partial_list.append(jnp.stack([corr_real, corr_imag]))
    partials = jnp.stack(partial_list)
    summed = lax.psum(partials, "grid")
    resid = residuals(inv_norm * summed, observed, amp_weight, pair_used)
    own_float = own_block.astype(jnp.float32)
    fields = jnp.zeros((2 * row_count, col_count), jnp.float32)
    kernel_part = jnp.zeros((col_count,), jnp.float32)
    for offset in range(2):
        resid_block = build_block(resid[offset])
        later_term = jnp.dot(resid_block, near_blocks[offset], preferred_element_type=jnp.float32)
        kernel_part = kernel_part + jnp.sum(own_float * later_term, axis=0)
        fields = fields + later_term
    for offset in range(2):
        resid_block = build_block(resid[offset])
        early_term = lax.dot_general(
            resid_block, own_block, (((0,), (0,)), ((), ())), preferred_element_type=jnp.float32
        )
        fields = fields + shifted(early_term, "cable", -(offset + 1))
    kernel = lax.psum(kernel_part, "cable") * kernel_scale
    adjoint = (inv_norm * source_weight[None, :] * fields).reshape(2, row_count, col_count)
    return (adjoint, kernel)


def solution(mesh):
    in_specs = (
        P(None, "cable", "grid"),
        P("grid"),
        P(None, None, "cable", None),
        P(None, "cable", None),
        P("cable", None),
    )
    out_specs = (P(None, "cable", "grid"), P("grid"))
    return jax.shard_map(shards, mesh=mesh, in_specs=in_specs, out_specs=out_specs, check_vma=False)
```

profile of v0, /device:TPU:1, one launch (start us, length us, event | category | flops | bytes accessed | tf_op | source)
XLA Modules:
  0.0 386.9 jit_solution(2514229055779088914)
XLA Ops:
  7.2 0.0 all-reduce.2.cloned.1.call-start
  7.2 0.0 copy-start
  7.2 0.0 copy-start.6
  7.2 3.1 collective-permute-start
  10.3 1.6 collective-permute-start.1
  12.0 43.5 %collective-permute-done = bf16[512,2048]{1,0:T(8,128)(2,1)S(1)} collective-permute-done((bf16[512,2048]{1,0:T(8,128)(2,1)}, bf16[512,2048]{1,0:T(8,128)(2,1)S(1)}, u32[]{:S(2)}, u32[]{:S(2)}) %collective-permute-start) | collective-permute-done | bytes 2097184 | tf_op jit(solution)/shard_map/ppermute | solution.py:11
  55.4 0.0 copy-start.1
  55.4 3.6 fusion.5
  59.1 0.0 copy-done.1
  59.1 0.1 fusion.10
  59.2 24.1 %collective-permute-done.1 = bf16[512,2048]{1,0:T(8,128)(2,1)S(1)} collective-permute-done((bf16[512,2048]{1,0:T(8,128)(2,1)}, bf16[512,2048]{1,0:T(8,128)(2,1)S(1)}, u32[]{:S(2)}, u32[]{:S(2)}) %collective-permute-start.1) | collective-permute-done | bytes 2097184 | tf_op jit(solution)/shard_map/ppermute | solution.py:11
  83.3 0.0 copy-done
  83.3 0.0 copy-done.6
  83.3 0.0 copy-start.3
  83.3 1.3 fusion.3
  84.6 0.0 copy-done.3
  84.6 0.1 fusion.8
  84.7 0.1 maximum_bitcast_fusion
  84.8 0.0 copy-start.7
  84.8 0.0 copy-start.5
  84.8 1.1 pad_maximum_fusion
  85.9 0.0 all-reduce.2.cloned.1.call-update
  85.9 0.0 copy-done.7
  85.9 0.1 copy-done.5
  86.0 0.1 broadcast_multiply_fusion
  86.1 88.0 %all-reduce.2.cloned.1.call-done = f32[2,2,256,256]{3,2,1,0:T(8,128)} async-done(((f32[2,2,256,256]{3,2,1,0:T(8,128)}), f32[2,2,256,256]{3,2,1,0:T(8,128)}) %all-reduce.2.cloned.1.call-update) | async-done | bytes 1048592 | tf_op jit(solution)/shard_map/psum | solution.py:52
  174.1 1.7 multiply_convert_fusion
  175.9 1.3 fusion.13
  177.2 5.8 %collective-permute-start.2 = (f32[512,2048]{1,0:T(8,128)S(1)}, f32[512,2048]{1,0:T(8,128)S(1)}, u32[]{:S(2)}, u32[]{:S(2)}) collective-permute-start(f32[512,2048]{1,0:T(8,128)S(1)} %fusion.13), channel_id=1, source_target_pairs={{8,0},{16,8},{24,16},{32,24},{40,32},{48,40},{56,48},{64,56},{72,6... | collective-permute-start | bytes 12582920 | tf_op jit(solution)/shard_map/ppermute | solution.py:11
  182.9 0.0 copy-start.2
  182.9 1.3 fusion.11
  184.2 3.1 collective-permute-start.3
  187.4 0.0 copy-done.2
  187.4 0.0 copy-start.4
  187.4 1.3 fusion.14
  188.6 85.2 %collective-permute-done.2 = f32[512,2048]{1,0:T(8,128)S(1)} collective-permute-done((f32[512,2048]{1,0:T(8,128)S(1)}, f32[512,2048]{1,0:T(8,128)S(1)}, u32[]{:S(2)}, u32[]{:S(2)}) %collective-permute-start.2) | collective-permute-done | bytes 4194336 | tf_op jit(solution)/shard_map/ppermute | solution.py:11
  273.8 3.9 %collective-permute-done.3 = f32[512,2048]{1,0:T(8,128)S(1)} collective-permute-done((f32[512,2048]{1,0:T(8,128)S(1)}, f32[512,2048]{1,0:T(8,128)S(1)}, u32[]{:S(2)}, u32[]{:S(2)}) %collective-permute-start.3) | collective-permute-done | bytes 4194336 | tf_op jit(solution)/shard_map/ppermute | solution.py:11
  277.8 0.0 copy-done.4
  277.8 5.3 %fusion.2 = (f32[2048]{0:T(1024)S(1)}, f32[2048]{0:T(1024)S(1)}, f32[512,2048]{1,0:T(8,128)}) fusion(bf16[2,256,2048]{2,1,0:T(8,128)(2,1)S(1)} %copy-done, f32[512,2048]{1,0:T(8,128)S(1)} %fusion.14, f32[512,2048]{1,0:T(8,128)S(1)} %collective-permute-done.3, f32[512,2048]{1,0:T(8,128)S(1)} %collective-permute-done.2, ...), kind=kOutput, calls=%fused_computation.5 | convolution fusion | flops 1085272064 | bytes 21389312 | tf_op jit(solution)/shard_map/dot_general | solution.py:59
  283.1 96.4 %psum.15 = f32[2048]{0:T(1024)S(1)} all-reduce(f32[2048]{0:T(1024)S(1)} %add.27), channel_id=1, replica_groups=mesh['cable'=32,'grid'=8] {'cable'}, use_global_device_ids=true, to_apply=%region_3.0 | all-reduce | flops 2048 | bytes 16384 | tf_op jit(solution)/shard_map/psum | solution.py:68
  379.5 0.6 broadcast_multiply_fusion.1
  (5 shorter events, 0.1 us)
Async XLA Ops:
  7.2 166.9 %all-reduce.2.cloned.1.call-start = ((), (), s32[]{:S(2)}) async-start(), calls=%async_computation | async-start | bytes 2097152 | tf_op jit(solution)/shard_map/psum | solution.py:52
  7.2 76.1 %copy-start = (bf16[2,256,2048]{2,1,0:T(8,128)(2,1)S(1)}, bf16[2,256,2048]{2,1,0:T(8,128)(2,1)}, u32[]{:S(2)}) copy-start(bf16[2,256,2048]{2,1,0:T(8,128)(2,1)} %param.5) | copy-start | bytes 6291460
  7.2 76.1 %copy-start.6 = (f32[2048]{0:T(1024)S(1)}, f32[2048]{0:T(1024)}, u32[]{:S(2)}) copy-start(f32[2048]{0:T(1024)} %param.6) | copy-start | bytes 24580
  7.2 48.2 %collective-permute-start = (bf16[512,2048]{1,0:T(8,128)(2,1)}, bf16[512,2048]{1,0:T(8,128)(2,1)S(1)}, u32[]{:S(2)}, u32[]{:S(2)}) collective-permute-start(bf16[512,2048]{1,0:T(8,128)(2,1)} %bitcast.36), channel_id=1, source_target_pairs={{248,0},{0,8},{8,16},{16,24},{24,32},{32,40},{40,48},{48,56},{56,6... | collective-permute-start | bytes 6291464 | tf_op jit(solution)/shard_map/ppermute | solution.py:11
  10.3 73.0 %collective-permute-start.1 = (bf16[512,2048]{1,0:T(8,128)(2,1)}, bf16[512,2048]{1,0:T(8,128)(2,1)S(1)}, u32[]{:S(2)}, u32[]{:S(2)}) collective-permute-start(bf16[512,2048]{1,0:T(8,128)(2,1)} %bitcast.37), channel_id=1, source_target_pairs={{240,0},{248,8},{0,16},{8,24},{16,32},{24,40},{32,48},{40,56},{48,... | collective-permute-start | bytes 6291464 | tf_op jit(solution)/shard_map/ppermute | solution.py:11
  55.4 3.7 copy-start.1
  83.3 1.3 copy-start.3
  84.8 1.1 copy-start.7
  84.8 1.2 copy-start.5
  177.2 96.7 %collective-permute-start.2 = (f32[512,2048]{1,0:T(8,128)S(1)}, f32[512,2048]{1,0:T(8,128)S(1)}, u32[]{:S(2)}, u32[]{:S(2)}) collective-permute-start(f32[512,2048]{1,0:T(8,128)S(1)} %fusion.13), channel_id=1, source_target_pairs={{8,0},{16,8},{24,16},{32,24},{40,32},{48,40},{56,48},{64,56},{72,6... | collective-permute-start | bytes 12582920 | tf_op jit(solution)/shard_map/ppermute | solution.py:11
  182.9 4.4 %copy-start.2 = (bf16[512,2048]{1,0:T(8,128)(2,1)S(1)}, bf16[512,2048]{1,0:T(8,128)(2,1)}, u32[]{:S(2)}) copy-start(bf16[512,2048]{1,0:T(8,128)(2,1)} %copy-done.1) | copy-start | bytes 6291460
  184.2 93.5 %collective-permute-start.3 = (f32[512,2048]{1,0:T(8,128)S(1)}, f32[512,2048]{1,0:T(8,128)S(1)}, u32[]{:S(2)}, u32[]{:S(2)}) collective-permute-start(f32[512,2048]{1,0:T(8,128)S(1)} %fusion.11), channel_id=1, source_target_pairs={{16,0},{24,8},{32,16},{40,24},{48,32},{56,40},{64,48},{72,56},{80,... | collective-permute-start | bytes 12582920 | tf_op jit(solution)/shard_map/ppermute | solution.py:11
  187.4 90.4 %copy-start.4 = (bf16[512,2048]{1,0:T(8,128)(2,1)S(1)}, bf16[512,2048]{1,0:T(8,128)(2,1)}, u32[]{:S(2)}) copy-start(bf16[512,2048]{1,0:T(8,128)(2,1)} %copy-done.3) | copy-start | bytes 6291460
Sparse Core Ops, SparseCore 0:
  86.0 88.0 all-reduce.1
where the time goes:
time: 387 us
  waiting for transfers between devices  245 us (63%)
  blocking collectives  96.4 us (25%)
  between operations  14.2 us (4%)
  matrix products  14.1 us (4%)
  starting transfers between devices  13.7 us (4%)
    ppermute x4, waiting for transfers between devices, shifted(): return lax.ppermute(block, axis, route)  157 us
    psum x1, blocking collectives, shards(): kernel = lax.psum(kernel_part, 'cable') * kernel_scale  96.4 us
    psum x1, waiting for transfers between devices, shards(): summed = lax.psum(partials, 'grid')  88 us
    ppermute x4, starting transfers between devices, shifted(): return lax.ppermute(block, axis, route)  13.6 us
  transfers between devices with their start and end apart: 5, of which 5 were waited for; matrix products, arithmetic and copies ran while one was open for 2% of the time, Pallas kernels for 0%

commit v1 on v0

--- a/solution.py
+++ b/solution.py
@@ -65,7 +65,7 @@
             resid_block, own_block, (((0,), (0,)), ((), ())), preferred_element_type=jnp.float32
         )
         fields = fields + shifted(early_term, "cable", -(offset + 1))
-    kernel = lax.psum(kernel_part, "cable") * kernel_scale
+    kernel = jnp.sum(lax.all_gather(kernel_part, "cable"), axis=0) * kernel_scale
     adjoint = (inv_norm * source_weight[None, :] * fields).reshape(2, row_count, col_count)
     return (adjoint, kernel)
 

time: 387 us -> 367 us (0.948)
  blocking collectives: 96.4 us -> 76.5 us
    psum x1 -> x0, blocking collectives: 96.4 us -> none  [shards(): kernel = lax.psum(kernel_part, 'cable') * kernel_scale]
    all_gather x0 -> x1, blocking collectives: none -> 76.5 us  [shards(): lax.all_gather(kernel_part, 'cable')]
where the time goes in v1:
time: 367 us
  waiting for transfers between devices  245 us (67%)
  blocking collectives  76.5 us (21%)
  between operations  14.2 us (4%)
  matrix products  14.1 us (4%)
  starting transfers between devices  13.7 us (4%)
  other arithmetic  3.76 us (1%)
    ppermute x4, waiting for transfers between devices, shifted(): return lax.ppermute(block, axis, route)  157 us
    psum x1, waiting for transfers between devices, shards(): summed = lax.psum(partials, 'grid')  88 us
    all_gather x1, blocking collectives, shards(): lax.all_gather(kernel_part, 'cable')  76.5 us
    ppermute x4, starting transfers between devices, shifted(): return lax.ppermute(block, axis, route)  13.6 us
  transfers between devices with their start and end apart: 5, of which 5 were waited for; matrix products, arithmetic and copies ran while one was open for 2% of the time, Pallas kernels for 0%

profile of v1, /device:TPU:1, one launch (start us, length us, event | category | flops | bytes accessed | tf_op | source)
XLA Modules:
  0.0 367.1 jit_solution(15575863965295634467)
XLA Ops:
  7.2 0.0 all-reduce.2.cloned.1.call-start
  7.2 0.0 copy-start
  7.2 0.0 copy-start.6
  7.2 3.1 collective-permute-start
  10.3 1.6 collective-permute-start.1
  12.0 43.5 %collective-permute-done = bf16[512,2048]{1,0:T(8,128)(2,1)S(1)} collective-permute-done((bf16[512,2048]{1,0:T(8,128)(2,1)}, bf16[512,2048]{1,0:T(8,128)(2,1)S(1)}, u32[]{:S(2)}, u32[]{:S(2)}) %collective-permute-start) | collective-permute-done | bytes 2097184 | tf_op jit(solution)/shard_map/ppermute | solution.py:11
  55.4 0.0 copy-start.1
  55.4 3.6 fusion.5
  59.1 0.0 copy-done.1
  59.1 0.1 fusion.10
  59.2 24.1 %collective-permute-done.1 = bf16[512,2048]{1,0:T(8,128)(2,1)S(1)} collective-permute-done((bf16[512,2048]{1,0:T(8,128)(2,1)}, bf16[512,2048]{1,0:T(8,128)(2,1)S(1)}, u32[]{:S(2)}, u32[]{:S(2)}) %collective-permute-start.1) | collective-permute-done | bytes 2097184 | tf_op jit(solution)/shard_map/ppermute | solution.py:11
  83.3 0.0 copy-done
  83.3 0.0 copy-done.6
  83.3 0.0 copy-start.3
  83.3 1.3 fusion.3
  84.6 0.0 copy-done.3
  84.6 0.1 fusion.8
  84.7 0.1 maximum_bitcast_fusion
  84.8 0.0 copy-start.7
  84.8 0.0 copy-start.5
  84.8 1.1 pad_maximum_fusion
  85.9 0.0 all-reduce.2.cloned.1.call-update
  85.9 0.0 copy-done.7
  85.9 0.1 copy-done.5
  86.0 0.1 broadcast_multiply_fusion
  86.1 88.0 %all-reduce.2.cloned.1.call-done = f32[2,2,256,256]{3,2,1,0:T(8,128)} async-done(((f32[2,2,256,256]{3,2,1,0:T(8,128)}), f32[2,2,256,256]{3,2,1,0:T(8,128)}) %all-reduce.2.cloned.1.call-update) | async-done | bytes 1048592 | tf_op jit(solution)/shard_map/psum | solution.py:52
  174.1 1.7 multiply_convert_fusion
  175.9 1.3 fusion.13
  177.2 5.8 %collective-permute-start.2 = (f32[512,2048]{1,0:T(8,128)S(1)}, f32[512,2048]{1,0:T(8,128)S(1)}, u32[]{:S(2)}, u32[]{:S(2)}) collective-permute-start(f32[512,2048]{1,0:T(8,128)S(1)} %fusion.13), channel_id=1, source_target_pairs={{8,0},{16,8},{24,16},{32,24},{40,32},{48,40},{56,48},{64,56},{72,6... | collective-permute-start | bytes 12582920 | tf_op jit(solution)/shard_map/ppermute | solution.py:11
  182.9 0.0 copy-start.2
  182.9 1.3 fusion.11
  184.2 3.1 collective-permute-start.3
  187.4 0.0 copy-done.2
  187.4 0.0 copy-start.4
  187.4 1.3 fusion.14
  188.6 85.2 %collective-permute-done.2 = f32[512,2048]{1,0:T(8,128)S(1)} collective-permute-done((f32[512,2048]{1,0:T(8,128)S(1)}, f32[512,2048]{1,0:T(8,128)S(1)}, u32[]{:S(2)}, u32[]{:S(2)}) %collective-permute-start.2) | collective-permute-done | bytes 4194336 | tf_op jit(solution)/shard_map/ppermute | solution.py:11
  273.8 3.9 %collective-permute-done.3 = f32[512,2048]{1,0:T(8,128)S(1)} collective-permute-done((f32[512,2048]{1,0:T(8,128)S(1)}, f32[512,2048]{1,0:T(8,128)S(1)}, u32[]{:S(2)}, u32[]{:S(2)}) %collective-permute-start.3) | collective-permute-done | bytes 4194336 | tf_op jit(solution)/shard_map/ppermute | solution.py:11
  277.8 0.0 copy-done.4
  277.8 5.3 %fusion.2 = (f32[2048]{0:T(1024)S(1)}, f32[2048]{0:T(1024)S(1)}, f32[512,2048]{1,0:T(8,128)}) fusion(bf16[2,256,2048]{2,1,0:T(8,128)(2,1)S(1)} %copy-done, f32[512,2048]{1,0:T(8,128)S(1)} %fusion.14, f32[512,2048]{1,0:T(8,128)S(1)} %collective-permute-done.3, f32[512,2048]{1,0:T(8,128)S(1)} %collective-permute-done.2, ...), kind=kOutput, calls=%fused_computation.5 | convolution fusion | flops 1085272064 | bytes 21389312 | tf_op jit(solution)/shard_map/dot_general | solution.py:59
  283.1 76.5 %all-gather = f32[65536]{0:T(1024)S(1)} all-gather(f32[2048]{0:T(1024)S(1)} %add.35), channel_id=2, replica_groups=mesh['cable'=32,'grid'=8] {'cable'}, dimensions={0}, use_global_device_ids=true | all-gather | bytes 270336 | tf_op jit(solution)/shard_map/all_gather | solution.py:68
  359.7 0.6 broadcast_multiply_fusion.1
  (7 shorter events, 0.1 us)
Async XLA Ops:
  7.2 166.9 %all-reduce.2.cloned.1.call-start = ((), (), s32[]{:S(2)}) async-start(), calls=%async_computation | async-start | bytes 2097152 | tf_op jit(solution)/shard_map/psum | solution.py:52
  7.2 76.1 %copy-start = (bf16[2,256,2048]{2,1,0:T(8,128)(2,1)S(1)}, bf16[2,256,2048]{2,1,0:T(8,128)(2,1)}, u32[]{:S(2)}) copy-start(bf16[2,256,2048]{2,1,0:T(8,128)(2,1)} %param.5) | copy-start | bytes 6291460
  7.2 76.1 %copy-start.6 = (f32[2048]{0:T(1024)S(1)}, f32[2048]{0:T(1024)}, u32[]{:S(2)}) copy-start(f32[2048]{0:T(1024)} %param.6) | copy-start | bytes 24580
  7.2 48.2 %collective-permute-start = (bf16[512,2048]{1,0:T(8,128)(2,1)}, bf16[512,2048]{1,0:T(8,128)(2,1)S(1)}, u32[]{:S(2)}, u32[]{:S(2)}) collective-permute-start(bf16[512,2048]{1,0:T(8,128)(2,1)} %bitcast.36), channel_id=1, source_target_pairs={{248,0},{0,8},{8,16},{16,24},{24,32},{32,40},{40,48},{48,56},{56,6... | collective-permute-start | bytes 6291464 | tf_op jit(solution)/shard_map/ppermute | solution.py:11
  10.3 73.0 %collective-permute-start.1 = (bf16[512,2048]{1,0:T(8,128)(2,1)}, bf16[512,2048]{1,0:T(8,128)(2,1)S(1)}, u32[]{:S(2)}, u32[]{:S(2)}) collective-permute-start(bf16[512,2048]{1,0:T(8,128)(2,1)} %bitcast.37), channel_id=1, source_target_pairs={{240,0},{248,8},{0,16},{8,24},{16,32},{24,40},{32,48},{40,56},{48,... | collective-permute-start | bytes 6291464 | tf_op jit(solution)/shard_map/ppermute | solution.py:11
  55.4 3.7 copy-start.1
  83.3 1.3 copy-start.3
  84.8 1.1 copy-start.7
  84.8 1.2 copy-start.5
  177.2 96.7 %collective-permute-start.2 = (f32[512,2048]{1,0:T(8,128)S(1)}, f32[512,2048]{1,0:T(8,128)S(1)}, u32[]{:S(2)}, u32[]{:S(2)}) collective-permute-start(f32[512,2048]{1,0:T(8,128)S(1)} %fusion.13), channel_id=1, source_target_pairs={{8,0},{16,8},{24,16},{32,24},{40,32},{48,40},{56,48},{64,56},{72,6... | collective-permute-start | bytes 12582920 | tf_op jit(solution)/shard_map/ppermute | solution.py:11
  182.9 4.4 %copy-start.2 = (bf16[512,2048]{1,0:T(8,128)(2,1)S(1)}, bf16[512,2048]{1,0:T(8,128)(2,1)}, u32[]{:S(2)}) copy-start(bf16[512,2048]{1,0:T(8,128)(2,1)} %copy-done.1) | copy-start | bytes 6291460
  184.2 93.5 %collective-permute-start.3 = (f32[512,2048]{1,0:T(8,128)S(1)}, f32[512,2048]{1,0:T(8,128)S(1)}, u32[]{:S(2)}, u32[]{:S(2)}) collective-permute-start(f32[512,2048]{1,0:T(8,128)S(1)} %fusion.11), channel_id=1, source_target_pairs={{16,0},{24,8},{32,16},{40,24},{48,32},{56,40},{64,48},{72,56},{80,... | collective-permute-start | bytes 12582920 | tf_op jit(solution)/shard_map/ppermute | solution.py:11
  187.4 90.4 %copy-start.4 = (bf16[512,2048]{1,0:T(8,128)(2,1)S(1)}, bf16[512,2048]{1,0:T(8,128)(2,1)}, u32[]{:S(2)}) copy-start(bf16[512,2048]{1,0:T(8,128)(2,1)} %copy-done.3) | copy-start | bytes 6291460
Sparse Core Ops, SparseCore 0:
  86.0 88.0 all-reduce.1
